TPU v7x, 32 devices: a whole 2x2x4 slice. The times are simulated.
32 devices in a mesh: fsdp: 8 (over y, x, core), sp: 4 (over z).
Axes of the slice: x: 2, y: 2, z: 4, core: 2. Of those that a mesh axis runs over, the one named last changes fastest.
Arguments:
- inputs: bfloat16 [16, 1024, 768], P('fsdp', 'sp'), may hold values from -6 to 6
- block_ids: int32 [16, 1024], P('fsdp', 'sp'), may hold values from 0 to 3, never falling along the last dimension, each value on 1 to 512 neighbouring positions
- first_gain: bfloat16 [768], P('fsdp'), may hold values from 0.5 to 1.5
- first_shift: bfloat16 [768], P('fsdp'), may hold values from -3 to 3
- w_project: bfloat16 [768, 2304], P('fsdp'), may hold values from -0.21875 to 0.21875
- query_bias: bfloat16 [768], P('fsdp'), may hold values from -3 to 3
- value_bias: bfloat16 [768], P('fsdp'), may hold values from -3 to 3
- w_output: bfloat16 [768, 768], P('fsdp'), may hold values from -4 to 4
- output_bias: bfloat16 [768], P('fsdp'), may hold values from -3 to 3
- second_gain: bfloat16 [768], P('fsdp'), may hold values from 0.5 to 1.5
- second_shift: bfloat16 [768], P('fsdp'), may hold values from -3 to 3
- w_expand: bfloat16 [768, 3072], P('fsdp'), may hold values from -0.21875 to 0.21875
- expand_bias: bfloat16 [3072], P('fsdp'), may hold values from -3 to 3
- w_reduce: bfloat16 [3072, 768], P('fsdp'), may hold values from -0.109375 to 0.109375
- reduce_bias: bfloat16 [768], P('fsdp'), may hold values from -3 to 3
- out_grad: bfloat16 [16, 1024, 768], P('fsdp', 'sp'), may hold values from -6 to 6
Outputs:
- layer_output: bfloat16 [16, 1024, 768], P('fsdp', 'sp')
- input_grad: float32 [16, 1024, 768], P('fsdp', 'sp')
- grad_first_gain: float32 [768], P('fsdp')
- grad_first_shift: float32 [768], P('fsdp')
- grad_project: float32 [768, 2304], P('fsdp')
- grad_query_bias: float32 [768], P('fsdp')
- grad_value_bias: float32 [768], P('fsdp')
- grad_output: float32 [768, 768], P('fsdp')
- grad_output_bias: float32 [768], P('fsdp')
- grad_second_gain: float32 [768], P('fsdp')
- grad_second_shift: float32 [768], P('fsdp')
- grad_expand: float32 [768, 3072], P('fsdp')
- grad_expand_bias: float32 [3072], P('fsdp')
- grad_reduce: float32 [3072, 768], P('fsdp')
- grad_reduce_bias: float32 [768], P('fsdp')
Inputs may be any that keep to these rules, and one draw needn't show every extreme that they name: `block_ids`: block numbers never fall along a sequence, and every number from 0 to 3 occurs in each sequence.
All inputs are finite; a program needn't handle non-finite values.
Results may differ from a plain program's by a relative error of at most 0.011.
Values may be sent and summed in bfloat16 or wider, within the bound.
No kernel may reach another device: no remote copies, remote signals or barrier semaphores. Data moves between devices by JAX's collectives and lax.ppermute only.
A program may use at most 192 MiB of HBM per device.

v0:
```python
import math
import jax
import jax.numpy as jnp
from jax import lax
from jax.sharding import PartitionSpec as P

H = 12
HD = 64
EPSILON = 1e-05
GELU_C = 0.7978845608028654
GELU_A = 0.044715
MASKED = -1e30


def norm_forward(rows, gain, shift):
    average = jnp.mean(rows, axis=-1, keepdims=True)
    centered = rows - average
    variance = jnp.mean(centered * centered, axis=-1, keepdims=True)
    inv_std = lax.rsqrt(variance + EPSILON)
    normed = centered * inv_std
    return (normed, inv_std, normed * gain + shift)


def norm_backward(grad_rows, normed, inv_std, gain):
    scaled = grad_rows * gain
    first_mean = jnp.mean(scaled, axis=-1, keepdims=True)
    second_mean = jnp.mean(scaled * normed, axis=-1, keepdims=True)
    grad_in = inv_std * (scaled - first_mean - normed * second_mean)
    return (grad_in, jnp.sum(grad_rows * normed, axis=0), jnp.sum(grad_rows, axis=0))


def gelu_parts(pre):
    tangent = jnp.tanh(GELU_C * (pre + GELU_A * pre * pre * pre))
    value = 0.5 * pre * (1.0 + tangent)
    slope = 0.5 * (1.0 + tangent) + 0.5 * pre * (1.0 - tangent * tangent) * GELU_C * (
        1.0 + 3.0 * GELU_A * pre * pre
    )
    return (value, slope)


def contract(left, right, left_dim, right_dim):
    return lax.dot_general(
        left, right, (((left_dim,), (right_dim,)), ((), ())), preferred_element_type=jnp.float32
    )


def masked_scores(query, keys, blocks, scale):
    raw = jnp.einsum("hdq,hdk->hqk", query, keys, preferred_element_type=jnp.float32) * scale
    allowed = blocks[None, :] <= blocks[:, None]
    return jnp.where(allowed[None], raw, MASKED)


def per_device(
    inputs,
    block_ids,
    first_gain,
    first_shift,
    w_project,
    query_bias,
    value_bias,
    w_output,
    output_bias,
    second_gain,
    second_shift,
    w_expand,
    expand_bias,
    w_reduce,
    reduce_bias,
    out_grad,
):
    seq_dev, local, width = inputs.shape
    rows = seq_dev * local
    groups = lax.axis_size("sp")
    per_dev = H // groups
    group_width = per_dev * HD
    length = local * groups
    scale = 1.0 / math.sqrt(HD)
    f32 = jnp.float32
    bf16 = jnp.bfloat16
    (
        gain_one,
        shift_one,
        proj_full,
        qbias_full,
        vbias_full,
        out_full,
        obias_full,
        gain_two,
        shift_two,
        exp_full,
        ebias_full,
        red_full,
        rbias_full,
    ) = (
        lax.all_gather(first_gain, "fsdp", axis=0, tiled=True),
        lax.all_gather(first_shift, "fsdp", axis=0, tiled=True),
        lax.all_gather(w_project, "fsdp", axis=0, tiled=True),
        lax.all_gather(query_bias, "fsdp", axis=0, tiled=True),
        lax.all_gather(value_bias, "fsdp", axis=0, tiled=True),
        lax.all_gather(w_output, "fsdp", axis=0, tiled=True),
        lax.all_gather(output_bias, "fsdp", axis=0, tiled=True),
        lax.all_gather(second_gain, "fsdp", axis=0, tiled=True),
        lax.all_gather(second_shift, "fsdp", axis=0, tiled=True),
        lax.all_gather(w_expand, "fsdp", axis=0, tiled=True),
        lax.all_gather(expand_bias, "fsdp", axis=0, tiled=True),
        lax.all_gather(w_reduce, "fsdp", axis=0, tiled=True),
        lax.all_gather(reduce_bias, "fsdp", axis=0, tiled=True),
    )
    blocks = lax.all_gather(block_ids, "sp", axis=1, tiled=True)
    resid = inputs.astype(f32).reshape(rows, width)
    normed_one, inv_one, pre_one = norm_forward(resid, gain_one.astype(f32), shift_one.astype(f32))
    normed_in = pre_one.astype(bf16)
    bias_all = jnp.concatenate([qbias_full, jnp.zeros_like(qbias_full), vbias_full]).astype(f32)
    proj_t = contract(proj_full, normed_in, 0, 1) + bias_all[:, None]
    proj_low = proj_t.astype(bf16).reshape(3, groups, group_width, seq_dev, local)
    heads = lax.all_to_all(proj_low, "sp", split_axis=1, concat_axis=4, tiled=True)
    per_seq = jnp.transpose(heads.reshape(3, per_dev, HD, seq_dev, length), (3, 0, 1, 2, 4))

    def attend(item):
        triple, seq_blocks = item
        scores = masked_scores(triple[0], triple[1], seq_blocks, scale)
        peak = jnp.max(scores, axis=-1, keepdims=True)
        raised = jnp.exp(scores - peak)
        summed = jnp.sum(raised, axis=-1, keepdims=True)
        attn_prob = (raised / summed).astype(bf16)
        mixed = jnp.einsum("hqk,hdk->hdq", attn_prob, triple[2], preferred_element_type=f32)
        return (mixed.astype(bf16), peak + jnp.log(summed))

    mixed_all, log_norm = lax.map(attend, (per_seq, blocks))
    mixed_t = jnp.transpose(mixed_all, (1, 2, 0, 3)).reshape(group_width, seq_dev, groups, local)
    attended = lax.all_to_all(mixed_t, "sp", split_axis=2, concat_axis=0, tiled=True).reshape(
        width, rows
    )
    middle = resid + (contract(attended, out_full, 0, 0) + obias_full.astype(f32))
    normed_two, inv_two, pre_two = norm_forward(middle, gain_two.astype(f32), shift_two.astype(f32))
    normed_mid = pre_two.astype(bf16)
    hidden = jnp.dot(normed_mid, exp_full, preferred_element_type=f32) + ebias_full.astype(f32)
    active_val, slope = gelu_parts(hidden)
    active = active_val.astype(bf16)
    result = middle + (
        jnp.dot(active, red_full, preferred_element_type=f32) + rbias_full.astype(f32)
    )
    layer_output = result.astype(bf16).reshape(seq_dev, local, width)
    gain_back, proj_back, out_back, gain_mid_back, exp_back, red_back = (
        lax.all_gather(first_gain, "fsdp", axis=0, tiled=True),
        lax.all_gather(w_project, "fsdp", axis=0, tiled=True),
        lax.all_gather(w_output, "fsdp", axis=0, tiled=True),
        lax.all_gather(second_gain, "fsdp", axis=0, tiled=True),
        lax.all_gather(w_expand, "fsdp", axis=0, tiled=True),
        lax.all_gather(w_reduce, "fsdp", axis=0, tiled=True),
    )
    grad_top = out_grad.reshape(rows, width)
    grad_red = contract(active, grad_top, 0, 0)
    grad_rbias = jnp.sum(grad_top, axis=0, dtype=f32)
    grad_active = contract(grad_top, red_back, 1, 1)
    grad_hidden = (grad_active * slope).astype(bf16)
    grad_exp = contract(normed_mid, grad_hidden, 0, 0)
    grad_ebias = jnp.sum(grad_hidden, axis=0, dtype=f32)
    grad_norm_two = contract(grad_hidden, exp_back, 1, 1)
    grad_mid_norm, grad_gain_two, grad_shift_two = norm_backward(
        grad_norm_two, normed_two, inv_two, gain_mid_back.astype(f32)
    )
    grad_middle = grad_top.astype(f32) + grad_mid_norm
    grad_branch = grad_middle.astype(bf16)
    grad_out = contract(attended, grad_branch, 1, 0)
    grad_obias = jnp.sum(grad_branch, axis=0, dtype=f32)
    grad_attn_t = (
        contract(out_back, grad_branch, 1, 1).astype(bf16).reshape(width, seq_dev, 1, local)
    )
    grad_heads = lax.all_to_all(grad_attn_t, "sp", split_axis=0, concat_axis=2, tiled=True)
    grad_seq = jnp.transpose(grad_heads.reshape(per_dev, HD, seq_dev, length), (2, 0, 1, 3))

    def attend_back(item):
        triple, seq_blocks, seq_norm, grad_mix = item
        scores = masked_scores(triple[0], triple[1], seq_blocks, scale)
        attn_prob = jnp.exp(scores - seq_norm)
        prob_low = attn_prob.astype(bf16)
        grad_values = jnp.einsum("hqk,hdq->hdk", prob_low, grad_mix, preferred_element_type=f32)
        grad_prob = jnp.einsum("hdq,hdk->hqk", grad_mix, triple[2], preferred_element_type=f32)
        centre = jnp.sum(grad_prob * attn_prob, axis=-1, keepdims=True)
        grad_scores = (attn_prob * (grad_prob - centre)).astype(bf16)
        grad_query = (
            jnp.einsum("hqk,hdk->hdq", grad_scores, triple[1], preferred_element_type=f32) * scale
        )
        grad_keys = (
            jnp.einsum("hqk,hdq->hdk", grad_scores, triple[0], preferred_element_type=f32) * scale
        )
        return jnp.stack([grad_query, grad_keys, grad_values]).astype(bf16)

    grad_triple = lax.map(attend_back, (per_seq, blocks, log_norm, grad_seq))
    grad_proj_heads = jnp.transpose(grad_triple, (1, 2, 3, 0, 4)).reshape(
        3, 1, group_width, seq_dev, length
    )
    grad_proj_t = lax.all_to_all(
        grad_proj_heads, "sp", split_axis=4, concat_axis=1, tiled=True
    ).reshape(3 * width, rows)
    grad_proj = contract(normed_in, grad_proj_t, 0, 1)
    grad_qbias = jnp.sum(grad_proj_t[:width], axis=1, dtype=f32)
    grad_vbias = jnp.sum(grad_proj_t[2 * width :], axis=1, dtype=f32)
    grad_norm_one = contract(grad_proj_t, proj_back, 0, 1)
    grad_in_norm, grad_gain_one, grad_shift_one = norm_backward(
        grad_norm_one, normed_one, inv_one, gain_back.astype(f32)
    )
    input_grad = (grad_middle + grad_in_norm).reshape(seq_dev, local, width)
    owned = (
        lax.psum_scatter(grad_gain_one, "fsdp", scatter_dimension=0, tiled=True),
        lax.psum_scatter(grad_shift_one, "fsdp", scatter_dimension=0, tiled=True),
        lax.psum_scatter(grad_proj, "fsdp", scatter_dimension=0, tiled=True),
        lax.psum_scatter(grad_qbias, "fsdp", scatter_dimension=0, tiled=True),
        lax.psum_scatter(grad_vbias, "fsdp", scatter_dimension=0, tiled=True),
        lax.psum_scatter(grad_out, "fsdp", scatter_dimension=0, tiled=True),
        lax.psum_scatter(grad_obias, "fsdp", scatter_dimension=0, tiled=True),
        lax.psum_scatter(grad_gain_two, "fsdp", scatter_dimension=0, tiled=True),
        lax.psum_scatter(grad_shift_two, "fsdp", scatter_dimension=0, tiled=True),
        lax.psum_scatter(grad_exp, "fsdp", scatter_dimension=0, tiled=True),
        lax.psum_scatter(grad_ebias, "fsdp", scatter_dimension=0, tiled=True),
        lax.psum_scatter(grad_red, "fsdp", scatter_dimension=0, tiled=True),
        lax.psum_scatter(grad_rbias, "fsdp", scatter_dimension=0, tiled=True),
    )
    (
        sum_gain_one,
        sum_shift_one,
        sum_proj,
        sum_qbias,
        sum_vbias,
        sum_out,
        sum_obias,
        sum_gain_two,
        sum_shift_two,
        sum_exp,
        sum_ebias,
        sum_red,
        sum_rbias,
    ) = lax.psum(
        (
            owned[0],
            owned[1],
            owned[2],
            owned[3],
            owned[4],
            owned[5],
            owned[6],
            owned[7],
            owned[8],
            owned[9],
            owned[10],
            owned[11],
            owned[12],
        ),
        "sp",
    )
    return (
        layer_output,
        input_grad,
        sum_gain_one,
        sum_shift_one,
        sum_proj,
        sum_qbias,
        sum_vbias,
        sum_out,
        sum_obias,
        sum_gain_two,
        sum_shift_two,
        sum_exp,
        sum_ebias,
        sum_red,
        sum_rbias,
    )


def solution(mesh):
    return jax.shard_map(
        per_device,
        mesh=mesh,
        in_specs=(
            P("fsdp", "sp", None),
            P("fsdp", "sp"),
            P("fsdp"),
            P("fsdp"),
            P("fsdp", None),
            P("fsdp"),
            P("fsdp"),
            P("fsdp", None),
            P("fsdp"),
            P("fsdp"),
            P("fsdp"),
            P("fsdp", None),
            P("fsdp"),
            P("fsdp", None),
            P("fsdp"),
            P("fsdp", "sp", None),
        ),
        out_specs=(
            P("fsdp", "sp", None),
            P("fsdp", "sp", None),
            P("fsdp"),
            P("fsdp"),
            P("fsdp", None),
            P("fsdp"),
            P("fsdp"),
            P("fsdp", None),
            P("fsdp"),
            P("fsdp"),
            P("fsdp"),
            P("fsdp", None),
            P("fsdp"),
            P("fsdp", None),
            P("fsdp"),
        ),
        check_vma=False,
    )
```

profile of v0, /device:TPU:0, one launch (start us, length us, event | category | flops | bytes accessed | tf_op | source)
XLA Modules:
  0.0 666.2 jit_solution(9742364295532393877)
XLA Ops:
  18.1 26.8 %all-reduce.20 = (bf16[768]{0:T(1024)(128)(2,1)S(1)}, bf16[768]{0:T(1024)(128)(2,1)S(1)}, bf16[768]{0:T(1024)(128)(2,1)S(1)}, bf16[768]{0:T(1024)(128)(2,1)S(1)}...) all-reduce(bf16[768]{0:T(1024)(128)(2,1)S(1)} %dynamic-update-slice, ...), channel_id=1, replica_groups=mesh['fsdp'=8,'sp'=4] {'fsdp'}, use_global_device_ids=true, to_apply=%add.1 | all-reduce | flops 6144 | bytes 24576
  49.3 5.4 fusion.47
  54.8 6.0 reshape.384
  60.8 6.2 copy.78
  72.5 56.1 %all_gather.53 = s32[2,1024]{1,0:T(2,128)S(1)} all-gather(s32[2,256]{1,0:T(2,128)S(1)} %copy-done.41), channel_id=1, replica_groups=mesh['fsdp'=8,'sp'=4] {'sp'}, dimensions={1}, use_global_device_ids=true | all-gather | bytes 10240 | tf_op jit(solution)/shard_map/all_gather | solution.py:109
  138.1 47.1 %while.22 = (s32[]{:T(128)}, bf16[2,3,64,1024]{3,2,1,0:T(8,128)(2,1)}, f32[2,3,1024,1]{2,1,3,0:T(4,128)S(1)}, bf16[2,3,3,64,1024]{4,3,2,1,0:T(8,128)(2,1)}, s32[...) while((s32[]{:T(128)}, bf16[2,3,64,1024]{3,2,1,0:T(8,128)(2,1)}, ...), condition=%wide.region_5.6_spmd, body=%wide.region_2.5_spmd.sunk | while | flops 844297216 | bytes 93973664 | solution.py:129
  152.1 9.5 %fusion.111 = bf16[2,3,64,1024]{3,2,1,0:T(8,128)(2,1)} fusion(bf16[2,3,64,1024]{3,2,1,0:T(8,128)(2,1)} %get-tuple-element.279, s32[]{:T(128)S(6)} %copy.119, f32[3,1024,1024]{1,2,0:T(8,128)} %copy-done.4, f32[3,1024]{1,0:T(4,128)S(1)} %fusion.110, f32[3,1024]{1,0:T(4,128)S(1)} %get-tuple-element.260, pred[1024,1024]{0,1:T(8,128)(4,1)} %broadcast_compare_fusion.4, ...), kind=kOutput, calls=%fused_computation.9.clone.1 | convolution fusion | flops 418578432 | bytes 14444032 | tf_op jit(solution)/shard_map/while/body/eval_jaxpr/hqk,hdk->hdq/dot_general | solution.py:126
  175.7 9.4 %fusion.111 = bf16[2,3,64,1024]{3,2,1,0:T(8,128)(2,1)} fusion(bf16[2,3,64,1024]{3,2,1,0:T(8,128)(2,1)} %get-tuple-element.279, s32[]{:T(128)S(6)} %copy.119, f32[3,1024,1024]{1,2,0:T(8,128)} %copy-done.4, f32[3,1024]{1,0:T(4,128)S(1)} %fusion.110, f32[3,1024]{1,0:T(4,128)S(1)} %get-tuple-element.260, pred[1024,1024]{0,1:T(8,128)(4,1)} %broadcast_compare_fusion.4, ...), kind=kOutput, calls=%fused_computation.9.clone.1 | convolution fusion | flops 418578432 | bytes 14444032 | tf_op jit(solution)/shard_map/while/body/eval_jaxpr/hqk,hdk->hdq/dot_general | solution.py:126
  192.5 9.3 %all-gather = bf16[8,1,384]{2,1,0:T(2,128)(2,1)S(1)} all-gather(bf16[1,1,384]{2,1,0:T(2,128)(2,1)S(1)} %reshape.365), channel_id=1, replica_groups=mesh['fsdp'=8,'sp'=4] {'fsdp'}, dimensions={0}, use_global_device_ids=true | all-gather | bytes 6912 | tf_op jit(solution)/shard_map/all_gather | solution.py:105
  201.8 6.2 all-to-all-done.1
  211.0 7.4 %fusion.72 = f32[512,3072]{1,0:T(8,128)} fusion(bf16[768,3072]{1,0:T(8,128)(2,1)} %all-gather.10.cloned.1.call-done, f32[512,768]{1,0:T(8,128)S(1)} %get-tuple-element.186, f32[768]{0:T(1024)S(1)} %convert_element_type.118, f32[768]{0:T(1024)S(1)} %convert_element_type.117, f32[512]{0:T(512)S(1)} %add_rsqrt_fusion, f32[512]{0:T(512)S(1)} %broadcast_multiply_fusion.4), kind=kOutput, calls=%fused_computation.120 | convolution fusion | flops 2417885184 | bytes 12593152 | tf_op jit(solution)/shard_map/dot_general | solution.py:137
  218.4 9.4 %convert_reduce_fusion = (f32[3072]{0:T(1024)}, bf16[512,3072]{1,0:T(8,128)(2,1)S(1)}) fusion(f32[512,3072]{1,0:T(8,128)} %fusion.72, f32[3072]{0:T(1024)S(1)} %bitcast.224, bf16[512,768]{1,0:T(8,128)(2,1)S(1)} %bitcast.210, bf16[3072,768]{1,0:T(8,128)(2,1)} %all-gather.12.cloned.1.call-done), kind=kOutput, calls=%fused_computation.64 | convolution fusion | flops 2450519040 | bytes 14966784 | tf_op jit(solution)/shard_map/dot_general | solution.py:42
  234.9 7.2 %fusion.71 = f32[768,3072]{1,0:T(8,128)} fusion(bf16[512,3072]{1,0:T(8,128)(2,1)} %copy-done.45, f32[512,768]{1,0:T(8,128)S(1)} %get-tuple-element.186, f32[768]{0:T(1024)S(1)} %convert_element_type.118, f32[768]{0:T(1024)S(1)} %convert_element_type.117, f32[512]{0:T(512)S(1)} %add_rsqrt_fusion, f32[512]{0:T(512)S(1)} %broadcast_multiply_fusion.4), kind=kOutput, calls=%fused_computation.119 | convolution fusion | flops 2417885184 | bytes 14166016 | tf_op jit(solution)/shard_map/dot_general | solution.py:42
  249.9 10.3 %fusion.73 = f32[3072,768]{1,0:T(8,128)} fusion(bf16[512,768]{1,0:T(8,128)(2,1)S(1)} %bitcast.211, f32[512,3072]{1,0:T(8,128)} %fusion.72, f32[3072]{0:T(1024)S(1)} %bitcast.225), kind=kOutput, calls=%fused_computation.121 | convolution fusion | flops 2431647744 | bytes 16527360 | tf_op jit(solution)/shard_map/dot_general | solution.py:42
  260.2 6.6 all-to-all-done.2
  268.1 75.5 %while.23 = (s32[]{:T(128)}, bf16[2,3,3,64,1024]{4,3,2,0,1:T(8,128)(2,1)}, bf16[2,3,3,64,1024]{4,3,2,1,0:T(8,128)(2,1)}, s32[2,1024]{1,0:T(2,128)S(1)}, f32[2,3,...) while((s32[]{:T(128)}, ...), condition=%wide.region_12.13_spmd, body=%wide.region_10.12_spmd.sunk | while | flops 2066019328 | bytes 260152704 | solution.py:190
  280.2 9.3 %multiply_reduce_fusion.7 = (f32[3,1024]{1,0:T(4,128)S(1)}, f32[3,1024,1024]{1,2,0:T(8,128)S(1)}) fusion(f32[3,1024,1024]{1,2,0:T(8,128)} %copy-done, f32[3,1024]{1,0:T(4,128)S(1)} %dynamic-slice_bitcast_fusion.26, pred[1024,1024]{0,1:T(8,128)(4,1)} %copy-done.3, bf16[2,3,3,64,1024]{4,3,2,1,0:T(8,128)(2,1)} %get-tuple-element.318, s32[]{:T(128)S(6)} %copy.127, ...), kind=kOutput, calls=%fused_computation.21.clone.1 | convolution fusion | flops 418378752 | bytes 27026944 | tf_op jit(solution)/shard_map/while/body/eval_jaxpr/hdq,hdk->hqk/dot_general | solution.py:179
  289.4 6.4 multiply_convert_fusion.5
  295.8 6.2 fusion.118
  318.1 9.9 %multiply_reduce_fusion.7 = (f32[3,1024]{1,0:T(4,128)S(1)}, f32[3,1024,1024]{1,2,0:T(8,128)S(1)}) fusion(f32[3,1024,1024]{1,2,0:T(8,128)} %copy-done, f32[3,1024]{1,0:T(4,128)S(1)} %dynamic-slice_bitcast_fusion.26, pred[1024,1024]{0,1:T(8,128)(4,1)} %copy-done.3, bf16[2,3,3,64,1024]{4,3,2,1,0:T(8,128)(2,1)} %get-tuple-element.318, s32[]{:T(128)S(6)} %copy.127, ...), kind=kOutput, calls=%fused_computation.21.clone.1 | convolution fusion | flops 418378752 | bytes 27026944 | tf_op jit(solution)/shard_map/while/body/eval_jaxpr/hdq,hdk->hqk/dot_general | solution.py:179
  328.0 6.4 multiply_convert_fusion.5
  334.4 5.2 fusion.118
  343.6 8.7 %copy.87 = bf16[3,1,192,2,1024]{2,3,0,1,4:T(2,128)(2,1)} copy(bf16[3,1,192,2,1024]{4,2,3,0,1:T(8,128)(2,1)} %bitcast.212) | data formatting | bytes 4718592 | tf_op jit(solution)/shard_map/reshape | solution.py:191
  358.5 68.2 %all-to-all-done.3 = bf16[3,1,192,2,1024]{2,3,0,1,4:T(2,128)(2,1)} async-done(((bf16[3,1,192,2,1024]{2,3,0,1,4:T(2,128)(2,1)}), bf16[3,1,192,2,1024]{2,3,0,1,4:T(2,128)(2,1)}, u32[]{:S(2)}, u32[]{:S(2)}) %all-to-all-start.3) | async-done | bytes 2359328 | tf_op jit(solution)/shard_map/all_to_all | solution.py:194
  426.6 8.5 %copy.98 = bf16[3,1,192,2,4,256]{5,4,2,3,0,1:T(4,128)(2,1)S(1)} copy(bf16[3,1,192,2,4,256]{2,3,0,5,4,1:T(2,128)(2,1)} %bitcast.34) | data formatting | bytes 4718592 | tf_op jit(solution)/shard_map/all_to_all | solution.py:194
  439.6 4.9 fusion.76
  444.7 71.6 %reduce-scatter.5.cloned.1.call-done = f32[96,2304]{1,0:T(8,128)} async-done(((f32[768,2304]{1,0:T(8,128)}), f32[96,2304]{1,0:T(8,128)}) %reduce-scatter.5.cloned.1.call-update) | async-done | bytes 884752 | tf_op jit(solution)/shard_map/reduce_scatter | solution.py:208
  519.0 9.4 %add_convert_fusion = bf16[512,768]{1,0:T(8,128)(2,1)} fusion(f32[512,768]{1,0:T(8,128)} %copy-done.13, bf16[3072,768]{1,0:T(8,128)(2,1)} %all-gather.12.cloned.1.call-done, f32[768]{0:T(1024)S(1)} %convert_element_type.122, f32[512,3072]{1,0:T(8,128)} %fusion.72, f32[3072]{0:T(1024)S(1)} %bitcast.226), kind=kOutput, calls=%fused_computation.98 | convolution fusion | flops 2432827392 | bytes 13384704 | tf_op jit(solution)/shard_map/dot_general | solution.py:141
  529.5 6.4 fusion.65
  535.9 25.0 %all-reduce.17 = (f32[768]{0:T(1024)S(1)}, f32[768]{0:T(1024)S(1)}, f32[768]{0:T(1024)S(1)}, f32[768]{0:T(1024)S(1)}, f32[768]{0:T(1024)S(1)}, /*index=5*/f32[76...) all-reduce(f32[768]{0:T(1024)S(1)} %get-tuple-element.113, ...), channel_id=2, replica_groups=mesh['fsdp'=8,'sp'=4] {'fsdp'}, use_global_device_ids=true, to_apply=%region_16.17.clone | all-reduce | flops 9216 | bytes 73728
  561.6 13.3 %all-reduce.18 = (f32[96]{0:T(128)}, f32[96]{0:T(128)}, f32[96]{0:T(128)}, f32[96]{0:T(128)}, f32[96]{0:T(128)}, /*index=5*/f32[96]{0:T(128)}, f32[96]{0:T(128)}, f32[384]{0:T(512)}, f32[96]{0:T(128)}) all-reduce(f32[96]{0:T(128)S(1)} %dynamic-slice.9, f32[96]{0:T(128)S(1)} %dynamic-slice.11, ...), channel_id=1, replica_groups=mesh['fsdp'=8,'sp'=4] {'sp'}, use_global_device_ids=true, to_apply=%region_17.18 | all-reduce | flops 1152 | bytes 9216 | tf_op jit(solution)/shard_map/psum | solution.py:234
  578.0 75.3 %all-reduce.23.cloned.1.call-done = (f32[96,2304]{1,0:T(8,128)}, f32[96,768]{1,0:T(8,128)}, f32[96,3072]{1,0:T(8,128)}, f32[384,768]{1,0:T(8,128)}) async-done(((f32[96,2304]{1,0:T(8,128)}, f32[96,768]{1,0:T(8,128)}, f32[96,3072]{1,0:T(8,128)}, f32[384,768]{1,0:T(8,128)}), (f32[96,2304]{1,0:T(8,128)}, f32[96,768]{1,0:T(8,128)}, f32[96,3072]{1,0:T(8,128)}, ...) | async-done | bytes 3538960 | tf_op jit(solution)/shard_map/psum | solution.py:234
  (245 shorter events, 138.6 us)
Async XLA Ops:
  7.2 41.8 %copy-start.5 = (bf16[2,256,768]{2,1,0:T(8,128)(2,1)S(1)}, bf16[2,256,768]{2,1,0:T(8,128)(2,1)}, u32[]{:S(2)}) copy-start(bf16[2,256,768]{2,1,0:T(8,128)(2,1)} %param.20) | copy-start | bytes 2359300
  7.2 42.1 %all-gather.6.cloned.1.call-start = ((), (), s32[]{:S(2)}) async-start(), calls=%async_computation.8 | async-start | bytes 3981312 | tf_op jit(solution)/shard_map/all_gather | solution.py:97
  7.9 200.3 %all-gather.8.cloned.1.call-start = ((), (), s32[]{:S(2)}) async-start(), calls=%async_computation.9 | async-start | bytes 1327104 | tf_op jit(solution)/shard_map/all_gather | solution.py:100
  8.7 202.4 %all-gather.10.cloned.1.call-start = ((), (), s32[]{:S(2)}) async-start(), calls=%async_computation.10 | async-start | bytes 5308416 | tf_op jit(solution)/shard_map/all_gather | solution.py:104
  66.9 61.7 %all-to-all-start = ((bf16[3,4,192,2,256]{4,3,2,0,1:T(2,128)(2,1)}), bf16[3,4,192,2,256]{4,3,2,0,1:T(2,128)(2,1)S(1)}, u32[]{:S(2)}, u32[]{:S(2)}) async-start(bf16[3,4,192,2,256]{4,3,2,0,1:T(2,128)(2,1)} %copy.78), calls=%async_computation | async-start | bytes 4718592 | tf_op jit(solution)/shard_map/all_to_all | solution.py:116
  71.9 146.6 %all-gather.12.cloned.1.call-start = ((), (), s32[]{:S(2)}) async-start(), calls=%async_computation.11 | async-start | bytes 5308416 | tf_op jit(solution)/shard_map/all_gather | solution.py:106
  185.2 7.3 %copy-start.43 = (bf16[384]{0:T(512)(128)(2,1)S(1)}, bf16[384]{0:T(512)(128)(2,1)}, u32[]{:S(2)}) copy-start(bf16[384]{0:T(512)(128)(2,1)} %param.32) | copy-start | bytes 2308
  185.2 23.0 %copy-start.6 = (bf16[2,256,768]{2,1,0:T(8,128)(2,1)S(1)}, bf16[2,256,768]{2,1,0:T(8,128)(2,1)}, u32[]{:S(2)}) copy-start(bf16[2,256,768]{2,1,0:T(8,128)(2,1)} %param.20) | copy-start | bytes 2359300
  188.9 19.1 %all-to-all-start.1 = ((bf16[192,2,4,256]{3,1,0,2:T(2,128)(2,1)}), bf16[192,2,4,256]{3,1,0,2:T(2,128)(2,1)S(1)}, u32[]{:S(2)}, u32[]{:S(2)}) async-start(bf16[192,2,4,256]{3,1,0,2:T(2,128)(2,1)} %copy.81), calls=%async_computation.1 | async-start | bytes 1572864 | tf_op jit(solution)/shard_map/all_to_all | solution.py:131
  192.4 252.2 %reduce-scatter.7.cloned.1.call-start = ((), (), s32[]{:S(2)}) async-start(), calls=%async_computation.13 | async-start | bytes 2654208 | tf_op jit(solution)/shard_map/reduce_scatter | solution.py:211
  201.8 48.0 %copy-start.35 = (f32[8,1,384]{2,1,0:T(1,128)}, f32[8,1,384]{2,1,0:T(1,128)S(1)}, u32[]{:S(2)}) copy-start(f32[8,1,384]{2,1,0:T(1,128)S(1)} %convert_element_type.136) | copy-start | bytes 36868
  210.7 24.2 %copy-start.13 = (f32[512,768]{1,0:T(8,128)}, f32[512,768]{1,0:T(8,128)S(1)}, u32[]{:S(2)}) copy-start(f32[512,768]{1,0:T(8,128)S(1)} %get-tuple-element.186) | copy-start | bytes 4718596
  211.0 7.4 %copy-start.17 = (bf16[2,256,768]{2,1,0:T(8,128)(2,1)S(1)}, bf16[2,256,768]{2,1,0:T(8,128)(2,1)}, u32[]{:S(2)}) copy-start(bf16[2,256,768]{2,1,0:T(8,128)(2,1)} %param.35) | copy-start | bytes 2359300
  218.4 9.4 %copy-start.44 = (bf16[768,3072]{1,0:T(8,128)(2,1)S(1)}, bf16[768,3072]{1,0:T(8,128)(2,1)}, u32[]{:S(2)}) copy-start(bf16[768,3072]{1,0:T(8,128)(2,1)} %all-gather.10.cloned.1.call-done) | copy-start | bytes 14155780
  232.6 9.5 %copy-start.8 = (f32[512,768]{1,0:T(8,128)}, f32[512,768]{1,0:T(8,128)S(1)}, u32[]{:S(2)}) copy-start(f32[512,768]{1,0:T(8,128)S(1)} %get-tuple-element.174) | copy-start | bytes 4718596
  234.8 209.8 %reduce-scatter.9.cloned.1.call-start = ((), (), s32[]{:S(2)}) async-start(), calls=%async_computation.14 | async-start | bytes 10616832 | tf_op jit(solution)/shard_map/reduce_scatter | solution.py:215
  242.1 7.7 %copy-start.19 = (bf16[2,256,768]{2,1,0:T(8,128)(2,1)S(1)}, bf16[2,256,768]{2,1,0:T(8,128)(2,1)}, u32[]{:S(2)}) copy-start(bf16[2,256,768]{2,1,0:T(8,128)(2,1)} %param.35) | copy-start | bytes 2359300
  246.1 20.6 %all-to-all-start.2 = ((bf16[768,2,1,256]{3,1,2,0:T(2,128)(2,1)}), bf16[768,2,1,256]{3,1,2,0:T(2,128)(2,1)S(1)}, u32[]{:S(2)}, u32[]{:S(2)}) async-start(bf16[768,2,1,256]{3,1,2,0:T(2,128)(2,1)} %copy.82), calls=%async_computation.2 | async-start | bytes 1572864 | tf_op jit(solution)/shard_map/all_to_all | solution.py:170
  249.6 195.1 %reduce-scatter.11.cloned.1.call-start = ((), (), s32[]{:S(2)}) async-start(), calls=%async_computation.15 | async-start | bytes 10616832 | tf_op jit(solution)/shard_map/reduce_scatter | solution.py:217
  280.2 9.3 %copy-start.1 = (f32[3,1024,1024]{1,2,0:T(8,128)S(1)}, f32[3,1024,1024]{1,2,0:T(8,128)}, u32[]{:S(2)}) copy-start(f32[3,1024,1024]{1,2,0:T(8,128)} %copy-done) | copy-start | bytes 37748740 | tf_op jit(solution)/shard_map/while
  318.1 9.9 %copy-start.1 = (f32[3,1024,1024]{1,2,0:T(8,128)S(1)}, f32[3,1024,1024]{1,2,0:T(8,128)}, u32[]{:S(2)}) copy-start(f32[3,1024,1024]{1,2,0:T(8,128)} %copy-done) | copy-start | bytes 37748740 | tf_op jit(solution)/shard_map/while
  352.3 74.3 %all-to-all-start.3 = ((bf16[3,1,192,2,1024]{2,3,0,1,4:T(2,128)(2,1)}), bf16[3,1,192,2,1024]{2,3,0,1,4:T(2,128)(2,1)}, u32[]{:S(2)}, u32[]{:S(2)}) async-start(bf16[3,1,192,2,1024]{2,3,0,1,4:T(2,128)(2,1)} %copy.87), calls=%async_computation.3 | async-start | bytes 6291456 | tf_op jit(solution)/shard_map/all_to_all | solution.py:194
  357.1 159.2 %reduce-scatter.5.cloned.1.call-start = ((), (), s32[]{:S(2)}) async-start(), calls=%async_computation.12 | async-start | bytes 7962624 | tf_op jit(solution)/shard_map/reduce_scatter | solution.py:208
  444.5 71.8 %copy-start.42 = (bf16[768]{0:T(1024)(128)(2,1)S(1)}, bf16[768]{0:T(1024)(128)(2,1)}, u32[]{:S(2)}) copy-start(bf16[768]{0:T(1024)(128)(2,1)} %get-tuple-element.170) | copy-start | bytes 4612
  444.5 74.4 %copy-start.36 = (f32[8,1,384]{2,1,0:T(1,128)S(1)}, f32[8,1,384]{2,1,0:T(1,128)}, u32[]{:S(2)}) copy-start(f32[8,1,384]{2,1,0:T(1,128)} %copy-done.35) | copy-start | bytes 36868
  444.6 208.7 %all-reduce.23.cloned.1.call-start = ((), (), s32[]{:S(2)}) async-start(), calls=%async_computation.16 | async-start | bytes 7077888 | tf_op jit(solution)/shard_map/psum | solution.py:234
  518.9 10.5 %copy-start.31 = (f32[1,2,2,128]{3,1,2,0:T(2,128)S(1)}, f32[1,2,2,128]{3,1,2,0:T(2,128)}, u32[]{:S(2)}) copy-start(f32[1,2,2,128]{3,1,2,0:T(2,128)} %copy-done.30) | copy-start | bytes 6148
  518.9 10.5 %copy-start.33 = (f32[1,2,2,128]{3,1,2,0:T(2,128)S(1)}, f32[1,2,2,128]{3,1,2,0:T(2,128)}, u32[]{:S(2)}) copy-start(f32[1,2,2,128]{3,1,2,0:T(2,128)} %copy-done.32) | copy-start | bytes 6148
  529.5 6.4 copy-start.34
  529.5 6.4 copy-start.37
  529.5 6.4 copy-start.39
  529.5 45.4 %copy-start.9 = (f32[512,768]{1,0:T(8,128)S(1)}, f32[512,768]{1,0:T(8,128)}, u32[]{:S(2)}) copy-start(f32[512,768]{1,0:T(8,128)} %copy-done.8) | copy-start | bytes 4718596
  (36 other events, 132.1 us)
Sparse Core Ops, SparseCore 0:
  9.9 36.7 all-gather.5
  48.5 23.9 all-gather.7
  74.4 38.7 all-gather.9
  114.9 38.7 all-gather.11
  235.0 44.5 reduce-scatter.6
  282.9 76.8 reduce-scatter.8
  363.2 76.8 reduce-scatter.10
  444.7 71.6 reduce-scatter.4
  518.9 134.2 all-reduce.22
where the time goes:
time: 673 us; the launch traced here: 666 us
  waiting for transfers between devices  231 us (34%)
  matrix products  147 us (22%)
  blocking collectives  130 us (19%)
  local copies, waits for them, and re-layouts  86.6 us (13%)
  other arithmetic  37.1 us (6%)
  starting transfers between devices  17.2 us (3%)
  between operations  16.8 us (2%)
    psum x1, waiting for transfers between devices, per_device(): lax.psum((owned[0], owned[1], owned[2], owned[3], owned[4], owned[5], own...  75.3 us
    reduce_scatter x1, waiting for transfers between devices, per_device(): lax.psum_scatter(grad_proj, 'fsdp', scatter_dimension=0, tiled=True)  71.6 us
    all_to_all x1, waiting for transfers between devices, per_device(): lax.all_to_all(grad_proj_heads, 'sp', split_axis=4, concat_axis=1, tiled=...  68.2 us
    all_gather x1, blocking collectives, per_device(): blocks = lax.all_gather(block_ids, 'sp', axis=1, tiled=True)  56.1 us
    dot_general x10, matrix products, contract(): lax.dot_general(left, right, (((left_dim,), (right_dim,)), ((), ())), pre...  54 us
    unnamed x2, blocking collectives  51.7 us
    while x36, local copies, waits for them, and re-layouts  20.6 us
    dot_general x2, matrix products, attend_back(): jnp.einsum('hdq,hdk->hqk', grad_mix, triple[2], preferred_element_type=f32)  19.1 us
  transfers between devices with their start and end apart: 13, of which 5 were waited for; matrix products, arithmetic and copies ran while one was open for 34% of the time, Pallas kernels for 0%

commit v1 on v0

--- a/solution.py
+++ b/solution.py
@@ -3,6 +3,7 @@
 import jax.numpy as jnp
 from jax import lax
 from jax.sharding import PartitionSpec as P
+from jax.lax import axis_index, axis_size, ppermute
 
 H = 12
 HD = 64
@@ -10,6 +11,13 @@
 GELU_C = 0.7978845608028654
 GELU_A = 0.044715
 MASKED = -1e30
+
+
+def tell_the_trails(xs, which_dim):
+    plain = list(xs.shape[1:])
+    plain[which_dim] *= xs.shape[0]
+    odd = jnp.moveaxis(xs, 0, which_dim).reshape(plain)
+    return odd
 
 
 def norm_forward(rows, gain, shift):
@@ -106,7 +114,14 @@
         lax.all_gather(w_reduce, "fsdp", axis=0, tiled=True),
         lax.all_gather(reduce_bias, "fsdp", axis=0, tiled=True),
     )
-    blocks = lax.all_gather(block_ids, "sp", axis=1, tiled=True)
+    axis_total = axis_size("sp")
+    history = tuple(((h, (h + 1) % axis_total) for h in range(axis_total)))
+    views = [block_ids]
+    while len(views) < axis_total:
+        views.append(ppermute(views[-1], "sp", history))
+    f_next = axis_index("sp")
+    views = jnp.stack(views)[(f_next - jnp.arange(axis_total)) % axis_total]
+    blocks = tell_the_trails(views, 1)
     resid = inputs.astype(f32).reshape(rows, width)
     normed_one, inv_one, pre_one = norm_forward(resid, gain_one.astype(f32), shift_one.astype(f32))
     normed_in = pre_one.astype(bf16)

time: 673 us -> 674 us (level)
  blocking collectives: 130 us -> 74.5 us
  waiting for transfers between devices: 231 us -> 271 us
  starting transfers between devices: 17.2 us -> 32.2 us
    all_gather x1 -> x0, blocking collectives: 56.1 us -> none  [per_device(): blocks = lax.all_gather(block_ids, 'sp', axis=1, tiled=True)]
    ppermute x0 -> x3, waiting for transfers between devices: none -> 42 us  [per_device(): views.append(ppermute(views[-1], 'sp', history))]
    ppermute x0 -> x3, starting transfers between devices: none -> 15 us  [per_device(): views.append(ppermute(views[-1], 'sp', history))]
  transfers between devices with their start and end apart: 13 -> 16, of which waited for: 5 -> 8; matrix products, arithmetic and copies ran while one was open for 34% -> 34% of each run, Pallas kernels for 0% -> 0%
where the time goes in v1:
time: 674 us; the launch traced here: 666 us
  waiting for transfers between devices  271 us (40%)
  matrix products  147 us (22%)
  local copies, waits for them, and re-layouts  87.1 us (13%)
  blocking collectives  74.5 us (11%)
  other arithmetic  37 us (5%)
  starting transfers between devices  32.2 us (5%)
  between operations  16.8 us (2%)
    psum x1, waiting for transfers between devices, per_device(): lax.psum((owned[0], owned[1], owned[2], owned[3], owned[4], owned[5], own...  75.3 us
    reduce_scatter x1, waiting for transfers between devices, per_device(): lax.psum_scatter(grad_proj, 'fsdp', scatter_dimension=0, tiled=True)  71.8 us
    all_to_all x1, waiting for transfers between devices, per_device(): lax.all_to_all(grad_proj_heads, 'sp', split_axis=4, concat_axis=1, tiled=...  68.1 us
    dot_general x10, matrix products, contract(): lax.dot_general(left, right, (((left_dim,), (right_dim,)), ((), ())), pre...  54.1 us
    unnamed x2, blocking collectives  51.7 us
    ppermute x3, waiting for transfers between devices, per_device(): views.append(ppermute(views[-1], 'sp', history))  42 us
    while x36, local copies, waits for them, and re-layouts  20.7 us
    dot_general x2, matrix products, attend_back(): jnp.einsum('hdq,hdk->hqk', grad_mix, triple[2], preferred_element_type=f32)  19 us
  transfers between devices with their start and end apart: 16, of which 8 were waited for; matrix products, arithmetic and copies ran while one was open for 34% of the time, Pallas kernels for 0%

profile of v1, /device:TPU:0, one launch (start us, length us, event | category | flops | bytes accessed | tf_op | source)
XLA Modules:
  0.0 666.4 jit_solution(5059913481879034670)
XLA Ops:
  18.1 26.8 %all-reduce.20 = (bf16[768]{0:T(1024)(128)(2,1)S(1)}, bf16[768]{0:T(1024)(128)(2,1)S(1)}, bf16[768]{0:T(1024)(128)(2,1)S(1)}, bf16[768]{0:T(1024)(128)(2,1)S(1)}...) all-reduce(bf16[768]{0:T(1024)(128)(2,1)S(1)} %dynamic-update-slice, ...), channel_id=1, replica_groups=mesh['fsdp'=8,'sp'=4] {'fsdp'}, use_global_device_ids=true, to_apply=%add.1 | all-reduce | flops 6144 | bytes 24576
  49.3 5.4 fusion.47
  54.7 6.0 reshape.445
  60.7 6.2 copy.78
  73.9 37.8 %collective-permute-done = s32[2,256]{1,0:T(2,128)S(1)} collective-permute-done((s32[2,256]{1,0:T(2,128)S(1)}, s32[2,256]{1,0:T(2,128)S(1)}, u32[]{:S(2)}, u32[]{:S(2)}) %collective-permute-start) | collective-permute-done | bytes 2080 | tf_op jit(solution)/shard_map/ppermute | solution.py:121
  111.7 10.3 %collective-permute-start.1 = (s32[2,256]{1,0:T(2,128)S(1)}, s32[2,256]{1,0:T(2,128)S(1)}, u32[]{:S(2)}, u32[]{:S(2)}) collective-permute-start(s32[2,256]{1,0:T(2,128)S(1)} %collective-permute-done), channel_id=1, source_target_pairs={{0,1},{1,2},{2,3},{3,0},{4,5},{5,6},{6,7},{7,4},{8,9},{9,10},{10,1... | collective-permute-start | bytes 6152 | tf_op jit(solution)/shard_map/ppermute | solution.py:121
  138.8 47.1 %while.22 = (s32[]{:T(128)}, bf16[2,3,64,1024]{3,2,1,0:T(8,128)(2,1)}, f32[2,3,1024,1]{2,1,3,0:T(4,128)S(1)}, bf16[2,3,3,64,1024]{4,3,2,1,0:T(8,128)(2,1)}, s32[...) while((s32[]{:T(128)}, bf16[2,3,64,1024]{3,2,1,0:T(8,128)(2,1)}, ...), condition=%wide.region_5.6_spmd, body=%wide.region_2.5_spmd.sunk | while | flops 844297216 | bytes 93973664 | solution.py:144
  152.9 9.4 %fusion.113 = bf16[2,3,64,1024]{3,2,1,0:T(8,128)(2,1)} fusion(bf16[2,3,64,1024]{3,2,1,0:T(8,128)(2,1)} %get-tuple-element.279, s32[]{:T(128)S(6)} %copy.119, f32[3,1024,1024]{1,2,0:T(8,128)} %copy-done.4, f32[3,1024]{1,0:T(4,128)S(1)} %fusion.112, f32[3,1024]{1,0:T(4,128)S(1)} %get-tuple-element.260, ...), kind=kOutput, calls=%fused_computation.10.clone.1 | convolution fusion | flops 418578432 | bytes 14444032 | tf_op jit(solution)/shard_map/while/body/eval_jaxpr/hqk,hdk->hdq/dot_general | solution.py:141
  176.4 9.4 %fusion.113 = bf16[2,3,64,1024]{3,2,1,0:T(8,128)(2,1)} fusion(bf16[2,3,64,1024]{3,2,1,0:T(8,128)(2,1)} %get-tuple-element.279, s32[]{:T(128)S(6)} %copy.119, f32[3,1024,1024]{1,2,0:T(8,128)} %copy-done.4, f32[3,1024]{1,0:T(4,128)S(1)} %fusion.112, f32[3,1024]{1,0:T(4,128)S(1)} %get-tuple-element.260, ...), kind=kOutput, calls=%fused_computation.10.clone.1 | convolution fusion | flops 418578432 | bytes 14444032 | tf_op jit(solution)/shard_map/while/body/eval_jaxpr/hqk,hdk->hdq/dot_general | solution.py:141
  193.3 9.4 %all-gather = bf16[8,1,384]{2,1,0:T(2,128)(2,1)S(1)} all-gather(bf16[1,1,384]{2,1,0:T(2,128)(2,1)S(1)} %reshape.426), channel_id=1, replica_groups=mesh['fsdp'=8,'sp'=4] {'fsdp'}, dimensions={0}, use_global_device_ids=true | all-gather | bytes 6912 | tf_op jit(solution)/shard_map/all_gather | solution.py:113
  202.7 5.6 all-to-all-done.1
  211.3 7.4 %fusion.74 = f32[512,3072]{1,0:T(8,128)} fusion(bf16[768,3072]{1,0:T(8,128)(2,1)} %all-gather.10.cloned.1.call-done, f32[512,768]{1,0:T(8,128)S(1)} %get-tuple-element.186, f32[768]{0:T(1024)S(1)} %convert_element_type.118, f32[768]{0:T(1024)S(1)} %convert_element_type.117, f32[512]{0:T(512)S(1)} %add_rsqrt_fusion, f32[512]{0:T(512)S(1)} %broadcast_multiply_fusion.4), kind=kOutput, calls=%fused_computation.129 | convolution fusion | flops 2417885184 | bytes 12593152 | tf_op jit(solution)/shard_map/dot_general | solution.py:152
  218.7 9.4 %convert_reduce_fusion = (f32[3072]{0:T(1024)}, bf16[512,3072]{1,0:T(8,128)(2,1)S(1)}) fusion(f32[512,3072]{1,0:T(8,128)} %fusion.74, f32[3072]{0:T(1024)S(1)} %bitcast.234, bf16[512,768]{1,0:T(8,128)(2,1)S(1)} %bitcast.219, bf16[3072,768]{1,0:T(8,128)(2,1)} %all-gather.12.cloned.1.call-done), kind=kOutput, calls=%fused_computation.65 | convolution fusion | flops 2450519040 | bytes 14966784 | tf_op jit(solution)/shard_map/dot_general | solution.py:50
  235.2 7.2 %fusion.73 = f32[768,3072]{1,0:T(8,128)} fusion(bf16[512,3072]{1,0:T(8,128)(2,1)} %copy-done.45, f32[512,768]{1,0:T(8,128)S(1)} %get-tuple-element.186, f32[768]{0:T(1024)S(1)} %convert_element_type.118, f32[768]{0:T(1024)S(1)} %convert_element_type.117, f32[512]{0:T(512)S(1)} %add_rsqrt_fusion, f32[512]{0:T(512)S(1)} %broadcast_multiply_fusion.4), kind=kOutput, calls=%fused_computation.128 | convolution fusion | flops 2417885184 | bytes 14166016 | tf_op jit(solution)/shard_map/dot_general | solution.py:50
  250.3 10.3 %fusion.75 = f32[3072,768]{1,0:T(8,128)} fusion(bf16[512,768]{1,0:T(8,128)(2,1)S(1)} %bitcast.220, f32[512,3072]{1,0:T(8,128)} %fusion.74, f32[3072]{0:T(1024)S(1)} %bitcast.235), kind=kOutput, calls=%fused_computation.130 | convolution fusion | flops 2431647744 | bytes 16527360 | tf_op jit(solution)/shard_map/dot_general | solution.py:50
  260.6 6.2 all-to-all-done.2
  268.1 75.4 %while.23 = (s32[]{:T(128)}, bf16[2,3,3,64,1024]{4,3,2,0,1:T(8,128)(2,1)}, bf16[2,3,3,64,1024]{4,3,2,1,0:T(8,128)(2,1)}, s32[2,1024]{1,0:T(2,128)S(1)}, f32[2,3,...) while((s32[]{:T(128)}, ...), condition=%wide.region_12.13_spmd, body=%wide.region_10.12_spmd.sunk | while | flops 2066019328 | bytes 260152704 | solution.py:205
  280.2 9.3 %multiply_reduce_fusion.7 = (f32[3,1024]{1,0:T(4,128)S(1)}, f32[3,1024,1024]{1,2,0:T(8,128)S(1)}) fusion(f32[3,1024,1024]{1,2,0:T(8,128)} %copy-done, f32[3,1024]{1,0:T(4,128)S(1)} %dynamic-slice_bitcast_fusion.26, pred[1024,1024]{0,1:T(8,128)(4,1)} %copy-done.3, bf16[2,3,3,64,1024]{4,3,2,1,0:T(8,128)(2,1)} %get-tuple-element.318, s32[]{:T(128)S(6)} %copy.127, ...), kind=kOutput, calls=%fused_computation.22.clone.1 | convolution fusion | flops 418378752 | bytes 27026944 | tf_op jit(solution)/shard_map/while/body/eval_jaxpr/hdq,hdk->hqk/dot_general | solution.py:194
  289.5 6.4 multiply_convert_fusion.5
  295.9 6.4 fusion.120
  318.3 9.7 %multiply_reduce_fusion.7 = (f32[3,1024]{1,0:T(4,128)S(1)}, f32[3,1024,1024]{1,2,0:T(8,128)S(1)}) fusion(f32[3,1024,1024]{1,2,0:T(8,128)} %copy-done, f32[3,1024]{1,0:T(4,128)S(1)} %dynamic-slice_bitcast_fusion.26, pred[1024,1024]{0,1:T(8,128)(4,1)} %copy-done.3, bf16[2,3,3,64,1024]{4,3,2,1,0:T(8,128)(2,1)} %get-tuple-element.318, s32[]{:T(128)S(6)} %copy.127, ...), kind=kOutput, calls=%fused_computation.22.clone.1 | convolution fusion | flops 418378752 | bytes 27026944 | tf_op jit(solution)/shard_map/while/body/eval_jaxpr/hdq,hdk->hqk/dot_general | solution.py:194
  328.0 6.4 multiply_convert_fusion.5
  334.4 5.2 fusion.120
  343.6 8.7 %copy.87 = bf16[3,1,192,2,1024]{2,3,0,1,4:T(2,128)(2,1)} copy(bf16[3,1,192,2,1024]{4,2,3,0,1:T(8,128)(2,1)} %bitcast.221) | data formatting | bytes 4718592 | tf_op jit(solution)/shard_map/reshape | solution.py:206
  358.4 68.1 %all-to-all-done.3 = bf16[3,1,192,2,1024]{2,3,0,1,4:T(2,128)(2,1)} async-done(((bf16[3,1,192,2,1024]{2,3,0,1,4:T(2,128)(2,1)}), bf16[3,1,192,2,1024]{2,3,0,1,4:T(2,128)(2,1)}, u32[]{:S(2)}, u32[]{:S(2)}) %all-to-all-start.3) | async-done | bytes 2359328 | tf_op jit(solution)/shard_map/all_to_all | solution.py:209
  426.6 8.6 %copy.98 = bf16[3,1,192,2,4,256]{5,4,2,3,0,1:T(4,128)(2,1)S(1)} copy(bf16[3,1,192,2,4,256]{2,3,0,5,4,1:T(2,128)(2,1)} %bitcast.42) | data formatting | bytes 4718592 | tf_op jit(solution)/shard_map/all_to_all | solution.py:209
  444.6 71.8 %reduce-scatter.5.cloned.1.call-done = f32[96,2304]{1,0:T(8,128)} async-done(((f32[768,2304]{1,0:T(8,128)}), f32[96,2304]{1,0:T(8,128)}) %reduce-scatter.5.cloned.1.call-update) | async-done | bytes 884752 | tf_op jit(solution)/shard_map/reduce_scatter | solution.py:223
  519.1 9.4 %add_convert_fusion = bf16[512,768]{1,0:T(8,128)(2,1)} fusion(f32[512,768]{1,0:T(8,128)} %copy-done.13, bf16[3072,768]{1,0:T(8,128)(2,1)} %all-gather.12.cloned.1.call-done, f32[768]{0:T(1024)S(1)} %convert_element_type.122, f32[512,3072]{1,0:T(8,128)} %fusion.74, f32[3072]{0:T(1024)S(1)} %bitcast.236), kind=kOutput, calls=%fused_computation.99 | convolution fusion | flops 2432827392 | bytes 13384704 | tf_op jit(solution)/shard_map/dot_general | solution.py:156
  529.7 6.4 fusion.65
  536.1 25.0 %all-reduce.17 = (f32[768]{0:T(1024)S(1)}, f32[768]{0:T(1024)S(1)}, f32[768]{0:T(1024)S(1)}, f32[768]{0:T(1024)S(1)}, f32[768]{0:T(1024)S(1)}, /*index=5*/f32[76...) all-reduce(f32[768]{0:T(1024)S(1)} %get-tuple-element.113, ...), channel_id=2, replica_groups=mesh['fsdp'=8,'sp'=4] {'fsdp'}, use_global_device_ids=true, to_apply=%region_16.17.clone | all-reduce | flops 9216 | bytes 73728
  561.7 13.3 %all-reduce.18 = (f32[96]{0:T(128)}, f32[96]{0:T(128)}, f32[96]{0:T(128)}, f32[96]{0:T(128)}, f32[96]{0:T(128)}, /*index=5*/f32[96]{0:T(128)}, f32[96]{0:T(128)}, f32[384]{0:T(512)}, f32[96]{0:T(128)}) all-reduce(f32[96]{0:T(128)S(1)} %dynamic-slice.9, f32[96]{0:T(128)S(1)} %dynamic-slice.11, ...), channel_id=1, replica_groups=mesh['fsdp'=8,'sp'=4] {'sp'}, use_global_device_ids=true, to_apply=%region_17.18 | all-reduce | flops 1152 | bytes 9216 | tf_op jit(solution)/shard_map/psum | solution.py:249
  578.2 75.3 %all-reduce.23.cloned.1.call-done = (f32[96,2304]{1,0:T(8,128)}, f32[96,768]{1,0:T(8,128)}, f32[96,3072]{1,0:T(8,128)}, f32[384,768]{1,0:T(8,128)}) async-done(((f32[96,2304]{1,0:T(8,128)}, f32[96,768]{1,0:T(8,128)}, f32[96,3072]{1,0:T(8,128)}, f32[384,768]{1,0:T(8,128)}), (f32[96,2304]{1,0:T(8,128)}, f32[96,768]{1,0:T(8,128)}, f32[96,3072]{1,0:T(8,128)}, ...) | async-done | bytes 3538960 | tf_op jit(solution)/shard_map/psum | solution.py:249
  (254 shorter events, 152.4 us)
Async XLA Ops:
  7.2 41.7 %copy-start.5 = (bf16[2,256,768]{2,1,0:T(8,128)(2,1)S(1)}, bf16[2,256,768]{2,1,0:T(8,128)(2,1)}, u32[]{:S(2)}) copy-start(bf16[2,256,768]{2,1,0:T(8,128)(2,1)} %param.20) | copy-start | bytes 2359300
  7.2 42.1 %all-gather.6.cloned.1.call-start = ((), (), s32[]{:S(2)}) async-start(), calls=%async_computation.8 | async-start | bytes 3981312 | tf_op jit(solution)/shard_map/all_gather | solution.py:105
  7.9 200.5 %all-gather.8.cloned.1.call-start = ((), (), s32[]{:S(2)}) async-start(), calls=%async_computation.9 | async-start | bytes 1327104 | tf_op jit(solution)/shard_map/all_gather | solution.py:108
  8.7 202.6 %all-gather.10.cloned.1.call-start = ((), (), s32[]{:S(2)}) async-start(), calls=%async_computation.10 | async-start | bytes 5308416 | tf_op jit(solution)/shard_map/all_gather | solution.py:112
  66.9 62.6 %all-to-all-start = ((bf16[3,4,192,2,256]{4,3,2,0,1:T(2,128)(2,1)}), bf16[3,4,192,2,256]{4,3,2,0,1:T(2,128)(2,1)S(1)}, u32[]{:S(2)}, u32[]{:S(2)}) async-start(bf16[3,4,192,2,256]{4,3,2,0,1:T(2,128)(2,1)} %copy.78), calls=%async_computation | async-start | bytes 4718592 | tf_op jit(solution)/shard_map/all_to_all | solution.py:131
  71.8 146.9 %all-gather.12.cloned.1.call-start = ((), (), s32[]{:S(2)}) async-start(), calls=%async_computation.11 | async-start | bytes 5308416 | tf_op jit(solution)/shard_map/all_gather | solution.py:114
  71.8 39.8 %collective-permute-start = (s32[2,256]{1,0:T(2,128)S(1)}, s32[2,256]{1,0:T(2,128)S(1)}, u32[]{:S(2)}, u32[]{:S(2)}) collective-permute-start(s32[2,256]{1,0:T(2,128)S(1)} %copy-done.42), channel_id=1, source_target_pairs={{0,1},{1,2},{2,3},{3,0},{4,5},{5,6},{6,7},{7,4},{8,9},{9,10},{10,1... | collective-permute-start | bytes 6152 | tf_op jit(solution)/shard_map/ppermute | solution.py:121
  111.7 11.7 %collective-permute-start.1 = (s32[2,256]{1,0:T(2,128)S(1)}, s32[2,256]{1,0:T(2,128)S(1)}, u32[]{:S(2)}, u32[]{:S(2)}) collective-permute-start(s32[2,256]{1,0:T(2,128)S(1)} %collective-permute-done), channel_id=1, source_target_pairs={{0,1},{1,2},{2,3},{3,0},{4,5},{5,6},{6,7},{7,4},{8,9},{9,10},{10,1... | collective-permute-start | bytes 6152 | tf_op jit(solution)/shard_map/ppermute | solution.py:121
  123.3 5.6 collective-permute-start.2
  185.9 7.4 %copy-start.43 = (bf16[384]{0:T(512)(128)(2,1)S(1)}, bf16[384]{0:T(512)(128)(2,1)}, u32[]{:S(2)}) copy-start(bf16[384]{0:T(512)(128)(2,1)} %param.32) | copy-start | bytes 2308
  185.9 22.6 %copy-start.6 = (bf16[2,256,768]{2,1,0:T(8,128)(2,1)S(1)}, bf16[2,256,768]{2,1,0:T(8,128)(2,1)}, u32[]{:S(2)}) copy-start(bf16[2,256,768]{2,1,0:T(8,128)(2,1)} %param.20) | copy-start | bytes 2359300
  189.6 18.6 %all-to-all-start.1 = ((bf16[192,2,4,256]{3,1,0,2:T(2,128)(2,1)}), bf16[192,2,4,256]{3,1,0,2:T(2,128)(2,1)S(1)}, u32[]{:S(2)}, u32[]{:S(2)}) async-start(bf16[192,2,4,256]{3,1,0,2:T(2,128)(2,1)} %copy.81), calls=%async_computation.1 | async-start | bytes 1572864 | tf_op jit(solution)/shard_map/all_to_all | solution.py:146
  193.2 251.4 %reduce-scatter.7.cloned.1.call-start = ((), (), s32[]{:S(2)}) async-start(), calls=%async_computation.13 | async-start | bytes 2654208 | tf_op jit(solution)/shard_map/reduce_scatter | solution.py:226
  202.7 47.6 %copy-start.35 = (f32[8,1,384]{2,1,0:T(1,128)}, f32[8,1,384]{2,1,0:T(1,128)S(1)}, u32[]{:S(2)}) copy-start(f32[8,1,384]{2,1,0:T(1,128)S(1)} %convert_element_type.136) | copy-start | bytes 36868
  210.9 24.2 %copy-start.13 = (f32[512,768]{1,0:T(8,128)}, f32[512,768]{1,0:T(8,128)S(1)}, u32[]{:S(2)}) copy-start(f32[512,768]{1,0:T(8,128)S(1)} %get-tuple-element.186) | copy-start | bytes 4718596
  211.3 7.4 %copy-start.17 = (bf16[2,256,768]{2,1,0:T(8,128)(2,1)S(1)}, bf16[2,256,768]{2,1,0:T(8,128)(2,1)}, u32[]{:S(2)}) copy-start(bf16[2,256,768]{2,1,0:T(8,128)(2,1)} %param.35) | copy-start | bytes 2359300
  218.7 9.4 %copy-start.44 = (bf16[768,3072]{1,0:T(8,128)(2,1)S(1)}, bf16[768,3072]{1,0:T(8,128)(2,1)}, u32[]{:S(2)}) copy-start(bf16[768,3072]{1,0:T(8,128)(2,1)} %all-gather.10.cloned.1.call-done) | copy-start | bytes 14155780
  232.9 9.5 %copy-start.8 = (f32[512,768]{1,0:T(8,128)}, f32[512,768]{1,0:T(8,128)S(1)}, u32[]{:S(2)}) copy-start(f32[512,768]{1,0:T(8,128)S(1)} %get-tuple-element.174) | copy-start | bytes 4718596
  235.1 209.5 %reduce-scatter.9.cloned.1.call-start = ((), (), s32[]{:S(2)}) async-start(), calls=%async_computation.14 | async-start | bytes 10616832 | tf_op jit(solution)/shard_map/reduce_scatter | solution.py:230
  242.4 7.8 %copy-start.19 = (bf16[2,256,768]{2,1,0:T(8,128)(2,1)S(1)}, bf16[2,256,768]{2,1,0:T(8,128)(2,1)}, u32[]{:S(2)}) copy-start(bf16[2,256,768]{2,1,0:T(8,128)(2,1)} %param.35) | copy-start | bytes 2359300
  246.5 20.4 %all-to-all-start.2 = ((bf16[768,2,1,256]{3,1,2,0:T(2,128)(2,1)}), bf16[768,2,1,256]{3,1,2,0:T(2,128)(2,1)S(1)}, u32[]{:S(2)}, u32[]{:S(2)}) async-start(bf16[768,2,1,256]{3,1,2,0:T(2,128)(2,1)} %copy.82), calls=%async_computation.2 | async-start | bytes 1572864 | tf_op jit(solution)/shard_map/all_to_all | solution.py:185
  250.0 194.6 %reduce-scatter.11.cloned.1.call-start = ((), (), s32[]{:S(2)}) async-start(), calls=%async_computation.15 | async-start | bytes 10616832 | tf_op jit(solution)/shard_map/reduce_scatter | solution.py:232
  280.2 9.3 %copy-start.1 = (f32[3,1024,1024]{1,2,0:T(8,128)S(1)}, f32[3,1024,1024]{1,2,0:T(8,128)}, u32[]{:S(2)}) copy-start(f32[3,1024,1024]{1,2,0:T(8,128)} %copy-done) | copy-start | bytes 37748740 | tf_op jit(solution)/shard_map/while
  318.3 9.7 %copy-start.1 = (f32[3,1024,1024]{1,2,0:T(8,128)S(1)}, f32[3,1024,1024]{1,2,0:T(8,128)}, u32[]{:S(2)}) copy-start(f32[3,1024,1024]{1,2,0:T(8,128)} %copy-done) | copy-start | bytes 37748740 | tf_op jit(solution)/shard_map/while
  352.3 74.3 %all-to-all-start.3 = ((bf16[3,1,192,2,1024]{2,3,0,1,4:T(2,128)(2,1)}), bf16[3,1,192,2,1024]{2,3,0,1,4:T(2,128)(2,1)}, u32[]{:S(2)}, u32[]{:S(2)}) async-start(bf16[3,1,192,2,1024]{2,3,0,1,4:T(2,128)(2,1)} %copy.87), calls=%async_computation.3 | async-start | bytes 6291456 | tf_op jit(solution)/shard_map/all_to_all | solution.py:209
  357.1 159.4 %reduce-scatter.5.cloned.1.call-start = ((), (), s32[]{:S(2)}) async-start(), calls=%async_computation.12 | async-start | bytes 7962624 | tf_op jit(solution)/shard_map/reduce_scatter | solution.py:223
  444.5 72.0 %copy-start.41 = (bf16[768]{0:T(1024)(128)(2,1)S(1)}, bf16[768]{0:T(1024)(128)(2,1)}, u32[]{:S(2)}) copy-start(bf16[768]{0:T(1024)(128)(2,1)} %get-tuple-element.170) | copy-start | bytes 4612
  444.5 74.6 %copy-start.36 = (f32[8,1,384]{2,1,0:T(1,128)S(1)}, f32[8,1,384]{2,1,0:T(1,128)}, u32[]{:S(2)}) copy-start(f32[8,1,384]{2,1,0:T(1,128)} %copy-done.35) | copy-start | bytes 36868
  444.5 208.9 %all-reduce.23.cloned.1.call-start = ((), (), s32[]{:S(2)}) async-start(), calls=%async_computation.16 | async-start | bytes 7077888 | tf_op jit(solution)/shard_map/psum | solution.py:249
  519.1 10.5 %copy-start.31 = (f32[1,2,2,128]{3,1,2,0:T(2,128)S(1)}, f32[1,2,2,128]{3,1,2,0:T(2,128)}, u32[]{:S(2)}) copy-start(f32[1,2,2,128]{3,1,2,0:T(2,128)} %copy-done.30) | copy-start | bytes 6148
  519.1 10.5 %copy-start.33 = (f32[1,2,2,128]{3,1,2,0:T(2,128)S(1)}, f32[1,2,2,128]{3,1,2,0:T(2,128)}, u32[]{:S(2)}) copy-start(f32[1,2,2,128]{3,1,2,0:T(2,128)} %copy-done.32) | copy-start | bytes 6148
  529.7 45.4 %copy-start.9 = (f32[512,768]{1,0:T(8,128)S(1)}, f32[512,768]{1,0:T(8,128)}, u32[]{:S(2)}) copy-start(f32[512,768]{1,0:T(8,128)} %copy-done.8) | copy-start | bytes 4718596
  (39 other events, 150.9 us)
Sparse Core Ops, SparseCore 0:
  9.9 36.7 all-gather.5
  48.5 23.9 all-gather.7
  74.4 38.7 all-gather.9
  114.9 38.7 all-gather.11
  235.2 44.9 reduce-scatter.6
  283.6 76.8 reduce-scatter.8
  363.9 76.8 reduce-scatter.10
  444.6 71.8 reduce-scatter.4
  519.1 134.2 all-reduce.22
